TPU v7x, 32 devices: a whole 2x2x4 slice. The times are simulated.
32 devices in a mesh: dp: 8 (over y, x, core), tensor: 4 (over z).
Axes of the slice: x: 2, y: 2, z: 4, core: 2. Of those that a mesh axis runs over, the one named last changes fastest.
Arguments:
- inputs: bfloat16 [2048, 2048], P(('dp', 'tensor')), parts along dimension 0, may hold values from -6 to 6
- grad_out: bfloat16 [2048, 2048], P(('dp', 'tensor')), parts along dimension 0, may hold values from -6 to 6
- gate_weight: bfloat16 [2048, 7168], P(None, 'tensor'), may hold values from -6 to 6
- up_weight: bfloat16 [2048, 7168], P(None, 'tensor'), may hold values from -6 to 6
- down_weight: bfloat16 [7168, 2048], P('tensor'), may hold values from -6 to 6
Outputs:
- grad_inputs: bfloat16 [2048, 2048], P(('dp', 'tensor')), parts along dimension 0
- grad_gate: bfloat16 [16384, 7168], P('dp', 'tensor'), parts along dimension 0
- grad_up: bfloat16 [16384, 7168], P('dp', 'tensor'), parts along dimension 0
- grad_down: bfloat16 [57344, 2048], P(('dp', 'tensor')), parts along dimension 0
There are 8 independent parts, one for each index of `dp`. A program takes and returns all parts, laid end to end along the dimension named above; an argument that names none is the same for every part. Nothing has to cross between parts.
All inputs are finite; a program needn't handle non-finite values.
Results may differ from a plain program's by a relative error of at most 0.0049.
Values may be sent and summed in bfloat16 or wider, within the bound.
A program may use at most 128 MiB of HBM per device.

v0:
```python
import jax
import jax.numpy as jnp
from jax import lax
from jax.sharding import PartitionSpec as P

D = 2048
FF = 7168


def contract_last(left, right):
    return lax.dot_general(
        left, right, (((1,), (1,)), ((), ())), preferred_element_type=jnp.float32
    )


def contract_first(left, right):
    return lax.dot_general(
        left, right, (((0,), (0,)), ((), ())), preferred_element_type=jnp.float32
    )


def on_device(inputs, grad_out, gate_weight, up_weight, down_weight):
    tokens_all = lax.all_gather(inputs, "tensor", axis=0, tiled=True)
    grads_all = lax.all_gather(grad_out, "tensor", axis=0, tiled=True)
    inv_width = D ** (-0.5)
    inv_rows = tokens_all.shape[0] ** (-0.5)
    inv_hidden = (2 * FF) ** (-0.5)
    gate = jnp.dot(tokens_all, gate_weight, preferred_element_type=jnp.float32) * inv_width
    up = jnp.dot(tokens_all, up_weight, preferred_element_type=jnp.float32) * inv_width
    sig = jax.nn.sigmoid(gate)
    act = gate * sig
    hidden = (act * up).astype(jnp.bfloat16)
    d_hidden = contract_last(grads_all, down_weight) * inv_width
    grad_down = (contract_first(hidden, grads_all) * inv_rows).astype(jnp.bfloat16)
    d_gate = (d_hidden * up * sig * (1.0 + gate * (1.0 - sig))).astype(jnp.bfloat16)
    d_up = (d_hidden * act).astype(jnp.bfloat16)
    grad_gate = (contract_first(tokens_all, d_gate) * inv_rows).astype(jnp.bfloat16)
    grad_up = (contract_first(tokens_all, d_up) * inv_rows).astype(jnp.bfloat16)
    summed = lax.psum_scatter(
        contract_last(d_gate, gate_weight) * inv_hidden
        + contract_last(d_up, up_weight) * inv_hidden,
        "tensor",
        scatter_dimension=0,
        tiled=True,
    )
    grad_inputs = summed.astype(jnp.bfloat16)
    return (grad_inputs, grad_gate, grad_up, grad_down)


def solution(mesh):
    placed = (
        P(("dp", "tensor"), None),
        P(("dp", "tensor"), None),
        P(None, "tensor"),
        P(None, "tensor"),
        P("tensor", None),
    )
    return jax.shard_map(
        on_device,
        mesh=mesh,
        in_specs=placed,
        out_specs=(
            P(("dp", "tensor"), None),
            P("dp", "tensor"),
            P("dp", "tensor"),
            P(("dp", "tensor"), None),
        ),
        check_vma=False,
    )
```

profile of v0, /device:TPU:0, one launch (start us, length us, event | category | flops | bytes accessed | tf_op | source)
XLA Modules:
  0.0 139.9 jit_solution(8619819542554499196)
XLA Ops:
  7.2 0.0 all-gather.5.cloned.1.call-start
  7.2 0.7 all-gather.5.cloned.1.call-update
  7.9 0.0 all-gather.3.cloned.1.call-start
  7.9 0.7 all-gather.3.cloned.1.call-update
  8.6 0.0 reduce-scatter.2.cloned.1.call-start
  8.7 31.5 %all-gather.5.cloned.1.call-done = bf16[256,2048]{1,0:T(8,128)(2,1)} async-done(((bf16[64,2048]{1,0:T(8,128)(2,1)}), bf16[256,2048]{1,0:T(8,128)(2,1)}) %all-gather.5.cloned.1.call-update) | async-done | bytes 1048592 | tf_op jit(solution)/shard_map/all_gather | solution.py:23
  40.2 0.0 copy-start
  40.2 6.8 %convolution_multiply_fusion = f32[256,1792]{1,0:T(8,128)} fusion(bf16[256,2048]{1,0:T(8,128)(2,1)} %all-gather.5.cloned.1.call-done, bf16[2048,1792]{1,0:T(8,128)(2,1)} %param.7), kind=kOutput, calls=%fused_computation.5 | convolution fusion | flops 1879506944 | bytes 10223616 | tf_op jit(solution)/shard_map/dot_general | solution.py:28
  47.0 0.0 copy-done
  47.0 6.6 %convolution_multiply_fusion.1 = f32[256,1792]{1,0:T(8,128)} fusion(bf16[256,2048]{1,0:T(8,128)(2,1)S(1)} %copy-done, bf16[2048,1792]{1,0:T(8,128)(2,1)} %param.8), kind=kOutput, calls=%fused_computation.6 | convolution fusion | flops 1879506944 | bytes 10223616 | tf_op jit(solution)/shard_map/dot_general | solution.py:29
  53.6 15.6 %all-gather.3.cloned.1.call-done = bf16[256,2048]{1,0:T(8,128)(2,1)} async-done(((bf16[64,2048]{1,0:T(8,128)(2,1)}), bf16[256,2048]{1,0:T(8,128)(2,1)}) %all-gather.3.cloned.1.call-update) | async-done | bytes 1048592 | tf_op jit(solution)/shard_map/all_gather | solution.py:24
  69.3 7.1 %multiply_convert_fusion.4 = (bf16[256,1792]{1,0:T(8,128)(2,1)S(1)}, bf16[256,1792]{1,0:T(8,128)(2,1)S(1)}) fusion(f32[256,1792]{1,0:T(8,128)} %convolution_multiply_fusion, f32[256,1792]{1,0:T(8,128)} %convolution_multiply_fusion.1, bf16[256,2048]{1,0:T(8,128)(2,1)} %all-gather.3.cloned.1.call-done, bf16[1792,2048]{1,0:T(8,128)(2,1)} %param.9), kind=kOutput, calls=%fused_computation.11 | convolution fusion | flops 1885470720 | bytes 13893632 | tf_op jit(solution)/shard_map/dot_general | solution.py:11
  76.3 5.2 %fusion.6 = f32[256,2048]{1,0:T(8,128)S(1)} fusion(bf16[256,1792]{1,0:T(8,128)(2,1)S(1)} %get-tuple-element.9, bf16[2048,1792]{1,0:T(8,128)(2,1)} %param.7), kind=kOutput, calls=%fused_computation.16 | convolution fusion | flops 1879048192 | bytes 10354688 | tf_op jit(solution)/shard_map/dot_general | solution.py:11
  81.5 6.6 %fusion.2 = f32[256,2048]{1,0:T(8,128)} fusion(f32[256,2048]{1,0:T(8,128)S(1)} %fusion.6, bf16[256,1792]{1,0:T(8,128)(2,1)S(1)} %get-tuple-element.8, bf16[2048,1792]{1,0:T(8,128)(2,1)} %param.8), kind=kOutput, calls=%fused_computation.9 | convolution fusion | flops 1880096768 | bytes 12451840 | tf_op jit(solution)/shard_map/dot_general | solution.py:11
  88.1 0.0 reduce-scatter.2.cloned.1.call-update
  88.1 5.2 %fusion.1 = bf16[2048,1792]{0,1:T(8,128)(2,1)} fusion(bf16[256,1792]{1,0:T(8,128)(2,1)S(1)} %get-tuple-element.8, bf16[256,2048]{1,0:T(8,128)(2,1)S(1)} %copy-done), kind=kOutput, calls=%fused_computation.4 | convolution fusion | flops 1886388224 | bytes 9306112 | tf_op jit(solution)/shard_map/dot_general | solution.py:17
  93.2 10.1 %copy.10 = bf16[2048,1792]{1,0:T(8,128)(2,1)} copy(bf16[2048,1792]{0,1:T(8,128)(2,1)} %fusion.1) | data formatting | bytes 14680064
  103.3 5.1 %fusion = bf16[2048,1792]{0,1:T(8,128)(2,1)} fusion(bf16[256,1792]{1,0:T(8,128)(2,1)S(1)} %get-tuple-element.9, bf16[256,2048]{1,0:T(8,128)(2,1)S(1)} %copy-done), kind=kOutput, calls=%fused_computation.3 | convolution fusion | flops 1886388224 | bytes 9306112 | tf_op jit(solution)/shard_map/dot_general | solution.py:17
  108.5 10.1 %copy.9 = bf16[2048,1792]{1,0:T(8,128)(2,1)} copy(bf16[2048,1792]{0,1:T(8,128)(2,1)} %fusion) | data formatting | bytes 14680064
  118.6 0.0 copy-done.1
  118.6 0.0 copy-done.2
  118.6 6.8 %multiply_convert_fusion = bf16[1792,2048]{1,0:T(8,128)(2,1)} fusion(bf16[256,2048]{1,0:T(8,128)(2,1)S(1)} %copy-done.1, f32[256,1792]{1,0:T(8,128)} %convolution_multiply_fusion.1, f32[256,1792]{1,0:T(8,128)S(1)} %copy-done.2), kind=kOutput, calls=%fused_computation | convolution fusion | flops 1889140736 | bytes 12058624 | tf_op jit(solution)/shard_map/dot_general | solution.py:17
  125.4 6.2 %reduce-scatter.2.cloned.1.call-done = f32[64,2048]{1,0:T(8,128)} async-done(((f32[256,2048]{1,0:T(8,128)}), f32[64,2048]{1,0:T(8,128)}) %reduce-scatter.2.cloned.1.call-update) | async-done | bytes 524304 | tf_op jit(solution)/shard_map/reduce_scatter | solution.py:39
  131.6 1.8 %convert_element_type.29 = bf16[64,2048]{1,0:T(8,128)(2,1)} convert(f32[64,2048]{1,0:T(8,128)} %reduce-scatter.2.cloned.1.call-done) | non-fusion elementwise | flops 131072 | bytes 786432 | tf_op jit(solution)/shard_map/convert_element_type | solution.py:46
  (2 shorter events, 0.0 us)
Async XLA Ops:
  7.2 33.1 %all-gather.5.cloned.1.call-start = ((), (), s32[]{:S(2)}) async-start(), calls=%async_computation.2 | async-start | bytes 1310720 | tf_op jit(solution)/shard_map/all_gather | solution.py:23
  7.9 61.4 %all-gather.3.cloned.1.call-start = ((), (), s32[]{:S(2)}) async-start(), calls=%async_computation.1 | async-start | bytes 1310720 | tf_op jit(solution)/shard_map/all_gather | solution.py:24
  8.6 122.9 %reduce-scatter.2.cloned.1.call-start = ((), (), s32[]{:S(2)}) async-start(), calls=%async_computation.3 | async-start | bytes 2621440 | tf_op jit(solution)/shard_map/reduce_scatter | solution.py:39
  40.2 6.8 %copy-start = (bf16[256,2048]{1,0:T(8,128)(2,1)S(1)}, bf16[256,2048]{1,0:T(8,128)(2,1)}, u32[]{:S(2)}) copy-start(bf16[256,2048]{1,0:T(8,128)(2,1)} %all-gather.5.cloned.1.call-done) | copy-start | bytes 3145732
  108.5 10.1 %copy-start.1 = (bf16[256,2048]{1,0:T(8,128)(2,1)S(1)}, bf16[256,2048]{1,0:T(8,128)(2,1)}, u32[]{:S(2)}) copy-start(bf16[256,2048]{1,0:T(8,128)(2,1)} %all-gather.3.cloned.1.call-done) | copy-start | bytes 3145732
  108.5 10.1 %copy-start.2 = (f32[256,1792]{1,0:T(8,128)S(1)}, f32[256,1792]{1,0:T(8,128)}, u32[]{:S(2)}) copy-start(f32[256,1792]{1,0:T(8,128)} %convolution_multiply_fusion) | copy-start | bytes 5505028
Sparse Core Ops, SparseCore 0:
  9.6 30.6 all-gather.4
  41.8 27.4 all-gather.2
  88.2 43.3 reduce-scatter.1
where the time goes:
time: 141 us; the launch traced here: 140 us
  waiting for transfers between devices  54.7 us (39%)
  matrix products  49.3 us (35%)
  local copies, waits for them, and re-layouts  20.2 us (14%)
  between operations  13.8 us (10%)
  other arithmetic  1.77 us (1%)
    all_gather x1, waiting for transfers between devices, on_device(): tokens_all = lax.all_gather(inputs, 'tensor', axis=0, tiled=True)  31.5 us
    unnamed x8, local copies, waits for them, and re-layouts  20.2 us
    dot_general x3, matrix products, contract_last(): lax.dot_general(left, right, (((1,), (1,)), ((), ())), preferred_element_...  18.8 us
    dot_general x3, matrix products, contract_first(): lax.dot_general(left, right, (((0,), (0,)), ((), ())), preferred_element_...  17.1 us
    all_gather x1, waiting for transfers between devices, on_device(): grads_all = lax.all_gather(grad_out, 'tensor', axis=0, tiled=True)  15.6 us
    dot_general x1, matrix products, on_device(): jnp.dot(tokens_all, gate_weight, preferred_element_type=jnp.float32)  6.77 us
    dot_general x1, matrix products, on_device(): jnp.dot(tokens_all, up_weight, preferred_element_type=jnp.float32)  6.64 us
    reduce_scatter x1, waiting for transfers between devices, on_device(): lax.psum_scatter(contract_last(d_gate, gate_weight) * inv_hidden + contra...  6.19 us
  transfers between devices with their start and end apart: 3, of which 3 were waited for; matrix products, arithmetic and copies ran while one was open for 36% of the time, Pallas kernels for 0%

commit v1 on v0

--- a/solution.py
+++ b/solution.py
@@ -20,7 +20,16 @@
 
 
 def on_device(inputs, grad_out, gate_weight, up_weight, down_weight):
-    tokens_all = lax.all_gather(inputs, "tensor", axis=0, tiled=True)
+    ways = lax.axis_size("tensor")
+    up_2 = [(d, (d + 1) % ways) for d in range(ways)]
+    down = [(d, (d - 1) % ways) for d in range(ways)]
+    earlier, later = ([inputs], [inputs])
+    for _ in range(ways // 2):
+        earlier.append(lax.ppermute(earlier[-1], "tensor", up_2))
+    for _ in range((ways - 1) // 2):
+        later.append(lax.ppermute(later[-1], "tensor", down))
+    line = jnp.concatenate([*earlier[::-1], *later[1:]], axis=0)
+    tokens_all = jnp.roll(line, (lax.axis_index("tensor") - ways // 2) * inputs.shape[0], axis=0)
     grads_all = lax.all_gather(grad_out, "tensor", axis=0, tiled=True)
     inv_width = D ** (-0.5)
     inv_rows = tokens_all.shape[0] ** (-0.5)

time: 141 us -> 121 us (0.86)
  local copies, waits for them, and re-layouts: 20.2 us -> 1.15 us
  starting transfers between devices: 0.11 us -> 6.98 us
  waiting for transfers between devices: 54.7 us -> 50.5 us
  matrix products: 49.3 us -> 46.5 us
    all_gather x1 -> x0, waiting for transfers between devices: 31.5 us -> none  [on_device(): tokens_all = lax.all_gather(inputs, 'tensor', axis=0, tiled=True)]
    ppermute x0 -> x3, waiting for transfers between devices: none -> 21.4 us  [the longest x2 15.7 us: on_device(): earlier.append(lax.ppermute(earlier[-1], 'tensor', up_2))]
    reduce_scatter x1, waiting for transfers between devices: 6.19 us -> 26.4 us  [on_device(): lax.psum_scatter(contract_last(d_gate, gate_weight) * inv_hidden + contra...]
    unnamed x8 -> x25, local copies, waits for them, and re-layouts: 20.2 us -> 1.13 us
    all_gather x1, waiting for transfers between devices: 15.6 us -> 2.71 us  [on_device(): grads_all = lax.all_gather(grad_out, 'tensor', axis=0, tiled=True)]
    ppermute x0 -> x3, starting transfers between devices: none -> 6.9 us  [the longest x1 3.82 us: on_device(): later.append(lax.ppermute(later[-1], 'tensor', down))]
    dot_general x1, matrix products: 6.64 us -> 3.33 us  [on_device(): jnp.dot(tokens_all, up_weight, preferred_element_type=jnp.float32)]
  transfers between devices with their start and end apart: 3 -> 5, of which waited for: 3 -> 5; matrix products, arithmetic and copies ran while one was open for 36% -> 23% of each run, Pallas kernels for 0% -> 0%
where the time goes in v1:
time: 121 us
  waiting for transfers between devices  50.5 us (42%)
  matrix products  46.5 us (38%)
  between operations  14.2 us (12%)
  starting transfers between devices  6.98 us (6%)
  other arithmetic  1.77 us (1%)
    reduce_scatter x1, waiting for transfers between devices, on_device(): lax.psum_scatter(contract_last(d_gate, gate_weight) * inv_hidden + contra...  26.4 us
    dot_general x3, matrix products, contract_last(): lax.dot_general(left, right, (((1,), (1,)), ((), ())), preferred_element_...  19.4 us
    dot_general x3, matrix products, contract_first(): lax.dot_general(left, right, (((0,), (0,)), ((), ())), preferred_element_...  17.2 us
    ppermute x2, waiting for transfers between devices, on_device(): earlier.append(lax.ppermute(earlier[-1], 'tensor', up_2))  15.7 us
    dot_general x1, matrix products, on_device(): jnp.dot(tokens_all, gate_weight, preferred_element_type=jnp.float32)  6.57 us
    ppermute x1, waiting for transfers between devices, on_device(): later.append(lax.ppermute(later[-1], 'tensor', down))  5.73 us
    ppermute x1, starting transfers between devices, on_device(): later.append(lax.ppermute(later[-1], 'tensor', down))  3.82 us
    dot_general x1, matrix products, on_device(): jnp.dot(tokens_all, up_weight, preferred_element_type=jnp.float32)  3.33 us
  transfers between devices with their start and end apart: 5, of which 5 were waited for; matrix products, arithmetic and copies ran while one was open for 23% of the time, Pallas kernels for 0%

profile of v1, /device:TPU:0, one launch (start us, length us, event | category | flops | bytes accessed | tf_op | source)
XLA Modules:
  0.0 121.1 jit_solution(60469939136901588)
XLA Ops:
  7.2 0.0 copy-start
  7.2 0.0 all-gather.2.cloned.1.call-start
  7.2 3.1 %collective-permute-start = (bf16[64,2048]{1,0:T(8,128)(2,1)}, bf16[64,2048]{1,0:T(8,128)(2,1)S(1)}, u32[]{:S(2)}, u32[]{:S(2)}) collective-permute-start(bf16[64,2048]{1,0:T(8,128)(2,1)} %param.5), channel_id=1, source_target_pairs={{0,1},{1,2},{2,3},{3,0},{4,5},{5,6},{6,7},{7,4},{8,9},{9,10},{10,1... | collective-permute-start | bytes 786440 | tf_op jit(solution)/shard_map/ppermute | solution.py:28
  10.3 8.5 %collective-permute-done = bf16[64,2048]{1,0:T(8,128)(2,1)S(1)} collective-permute-done((bf16[64,2048]{1,0:T(8,128)(2,1)}, bf16[64,2048]{1,0:T(8,128)(2,1)S(1)}, u32[]{:S(2)}, u32[]{:S(2)}) %collective-permute-start) | collective-permute-done | bytes 262176 | tf_op jit(solution)/shard_map/ppermute | solution.py:28
  18.8 3.8 %collective-permute-start.2 = (bf16[64,2048]{1,0:T(8,128)(2,1)}, bf16[64,2048]{1,0:T(8,128)(2,1)S(1)}, u32[]{:S(2)}, u32[]{:S(2)}) collective-permute-start(bf16[64,2048]{1,0:T(8,128)(2,1)} %param.5), channel_id=1, source_target_pairs={{0,3},{1,0},{2,1},{3,2},{4,7},{5,4},{6,5},{7,6},{8,11},{9,8},{10,9... | collective-permute-start | bytes 786440 | tf_op jit(solution)/shard_map/ppermute | solution.py:30
  22.7 0.0 all-gather.2.cloned.1.call-update
  22.7 0.0 reduce-scatter.2.cloned.1.call-start
  22.8 7.1 %collective-permute-done.1 = bf16[64,2048]{1,0:T(8,128)(2,1)S(1)} collective-permute-done((bf16[64,2048]{1,0:T(8,128)(2,1)S(1)}, bf16[64,2048]{1,0:T(8,128)(2,1)S(1)}, u32[]{:S(2)}, u32[]{:S(2)}) %collective-permute-start.1) | collective-permute-done | bytes 262176 | tf_op jit(solution)/shard_map/ppermute | solution.py:28
  29.9 1.0 constant_dynamic-update-slice_fusion.5
  30.9 5.7 %collective-permute-done.2 = bf16[64,2048]{1,0:T(8,128)(2,1)S(1)} collective-permute-done((bf16[64,2048]{1,0:T(8,128)(2,1)}, bf16[64,2048]{1,0:T(8,128)(2,1)S(1)}, u32[]{:S(2)}, u32[]{:S(2)}) %collective-permute-start.2) | collective-permute-done | bytes 262176 | tf_op jit(solution)/shard_map/ppermute | solution.py:30
  36.8 0.0 slice-start
  36.8 0.0 slice-start.1
  36.8 6.6 %convolution_multiply_fusion = f32[256,1792]{1,0:T(8,128)} fusion(bf16[2048,1792]{1,0:T(8,128)(2,1)} %param.7, bf16[512,2048]{1,0:T(8,128)(2,1)S(1)} %constant_dynamic-update-slice_fusion, s32[]{:T(128)S(6)} %select_n.14), kind=kOutput, calls=%fused_computation.3 | convolution fusion | flops 1879506944 | bytes 10223620 | tf_op jit(solution)/shard_map/dot_general | solution.py:37
  43.4 3.3 %convolution_multiply_fusion.1 = f32[256,1792]{1,0:T(8,128)} fusion(bf16[2048,1792]{1,0:T(8,128)(2,1)S(1)} %bitcast.12, bf16[512,2048]{1,0:T(8,128)(2,1)S(1)} %constant_dynamic-update-slice_fusion, s32[]{:T(128)S(6)} %select_n.14), kind=kOutput, calls=%fused_computation.4 | convolution fusion | flops 1879506944 | bytes 10223620 | tf_op jit(solution)/shard_map/dot_general | solution.py:38
  46.7 2.7 %all-gather.2.cloned.1.call-done = bf16[256,2048]{1,0:T(8,128)(2,1)} async-done(((bf16[64,2048]{1,0:T(8,128)(2,1)}), bf16[256,2048]{1,0:T(8,128)(2,1)}) %all-gather.2.cloned.1.call-update) | async-done | bytes 1048592 | tf_op jit(solution)/shard_map/all_gather | solution.py:33
  49.4 7.1 %multiply_convert_fusion.4 = (bf16[256,1792]{1,0:T(8,128)(2,1)S(1)}, bf16[256,1792]{1,0:T(8,128)(2,1)S(1)}) fusion(f32[256,1792]{1,0:T(8,128)} %convolution_multiply_fusion, f32[256,1792]{1,0:T(8,128)} %convolution_multiply_fusion.1, bf16[256,2048]{1,0:T(8,128)(2,1)} %all-gather.2.cloned.1.call-done, bf16[1792,2048]{1,0:T(8,128)(2,1)} %param.9), kind=kOutput, calls=%fused_computation.9 | convolution fusion | flops 1885470720 | bytes 13893632 | tf_op jit(solution)/shard_map/dot_general | solution.py:11
  56.5 5.8 %fusion.12 = f32[256,2048]{1,0:T(8,128)S(1)} fusion(bf16[256,1792]{1,0:T(8,128)(2,1)S(1)} %get-tuple-element.5, bf16[2048,1792]{1,0:T(8,128)(2,1)} %param.7), kind=kOutput, calls=%fused_computation.30 | convolution fusion | flops 1879048192 | bytes 10354688 | tf_op jit(solution)/shard_map/dot_general | solution.py:11
  62.4 6.6 %fusion = f32[256,2048]{1,0:T(8,128)} fusion(f32[256,2048]{1,0:T(8,128)S(1)} %fusion.12, bf16[256,1792]{1,0:T(8,128)(2,1)S(1)} %get-tuple-element.4, bf16[2048,1792]{1,0:T(8,128)(2,1)} %param.8), kind=kOutput, calls=%fused_computation.7 | convolution fusion | flops 1880096768 | bytes 12451840 | tf_op jit(solution)/shard_map/dot_general | solution.py:11
  68.9 0.0 reduce-scatter.2.cloned.1.call-update
  69.0 6.4 %multiply_convert_fusion.1 = bf16[2048,1792]{1,0:T(8,128)(2,1)} fusion(bf16[256,1792]{1,0:T(8,128)(2,1)} %copy-done.2, bf16[512,2048]{1,0:T(8,128)(2,1)S(1)} %constant_dynamic-update-slice_fusion, s32[]{:T(128)S(6)} %select_n.14), kind=kOutput, calls=%fused_computation.1 | convolution fusion | flops 1886388224 | bytes 9306116 | tf_op jit(solution)/shard_map/dot_general | solution.py:17
  75.4 5.4 %multiply_convert_fusion.2 = bf16[2048,1792]{1,0:T(8,128)(2,1)} fusion(bf16[256,1792]{1,0:T(8,128)(2,1)S(1)} %copy-done.4, bf16[512,2048]{1,0:T(8,128)(2,1)S(1)} %constant_dynamic-update-slice_fusion, s32[]{:T(128)S(6)} %select_n.14), kind=kOutput, calls=%fused_computation.2 | convolution fusion | flops 1886388224 | bytes 9306116 | tf_op jit(solution)/shard_map/dot_general | solution.py:17
  80.8 5.3 %multiply_convert_fusion = bf16[1792,2048]{1,0:T(8,128)(2,1)} fusion(bf16[256,2048]{1,0:T(8,128)(2,1)S(1)} %copy-done.1, f32[256,1792]{1,0:T(8,128)S(1)} %copy-done.6, f32[256,1792]{1,0:T(8,128)S(1)} %copy-done.5), kind=kOutput, calls=%fused_computation | convolution fusion | flops 1889140736 | bytes 12058624 | tf_op jit(solution)/shard_map/dot_general | solution.py:17
  86.2 26.4 %reduce-scatter.2.cloned.1.call-done = f32[64,2048]{1,0:T(8,128)} async-done(((f32[256,2048]{1,0:T(8,128)}), f32[64,2048]{1,0:T(8,128)}) %reduce-scatter.2.cloned.1.call-update) | async-done | bytes 524304 | tf_op jit(solution)/shard_map/reduce_scatter | solution.py:48
  112.5 1.8 %convert_element_type.23 = bf16[64,2048]{1,0:T(8,128)(2,1)} convert(f32[64,2048]{1,0:T(8,128)} %reduce-scatter.2.cloned.1.call-done) | non-fusion elementwise | flops 131072 | bytes 786432 | tf_op jit(solution)/shard_map/convert_element_type | solution.py:55
  (24 shorter events, 0.2 us)
Async XLA Ops:
  7.2 29.6 %copy-start = (bf16[64,2048]{1,0:T(8,128)(2,1)S(1)}, bf16[64,2048]{1,0:T(8,128)(2,1)}, u32[]{:S(2)}) copy-start(bf16[64,2048]{1,0:T(8,128)(2,1)} %param.5) | copy-start | bytes 786436
  7.2 42.2 %all-gather.2.cloned.1.call-start = ((), (), s32[]{:S(2)}) async-start(), calls=%async_computation.1 | async-start | bytes 1310720 | tf_op jit(solution)/shard_map/all_gather | solution.py:33
  7.2 11.6 %collective-permute-start = (bf16[64,2048]{1,0:T(8,128)(2,1)}, bf16[64,2048]{1,0:T(8,128)(2,1)S(1)}, u32[]{:S(2)}, u32[]{:S(2)}) collective-permute-start(bf16[64,2048]{1,0:T(8,128)(2,1)} %param.5), channel_id=1, source_target_pairs={{0,1},{1,2},{2,3},{3,0},{4,5},{5,6},{6,7},{7,4},{8,9},{9,10},{10,1... | collective-permute-start | bytes 786440 | tf_op jit(solution)/shard_map/ppermute | solution.py:28
  18.8 11.0 %collective-permute-start.1 = (bf16[64,2048]{1,0:T(8,128)(2,1)S(1)}, bf16[64,2048]{1,0:T(8,128)(2,1)S(1)}, u32[]{:S(2)}, u32[]{:S(2)}) collective-permute-start(bf16[64,2048]{1,0:T(8,128)(2,1)S(1)} %collective-permute-done), channel_id=1, source_target_pairs={{0,1},{1,2},{2,3},{3,0},{4,5},{5,6},{6,7},{7,4},{8,9},{9,10},{10,1... | collective-permute-start | bytes 786440 | tf_op jit(solution)/shard_map/ppermute | solution.py:28
  18.8 17.8 %collective-permute-start.2 = (bf16[64,2048]{1,0:T(8,128)(2,1)}, bf16[64,2048]{1,0:T(8,128)(2,1)S(1)}, u32[]{:S(2)}, u32[]{:S(2)}) collective-permute-start(bf16[64,2048]{1,0:T(8,128)(2,1)} %param.5), channel_id=1, source_target_pairs={{0,3},{1,0},{2,1},{3,2},{4,7},{5,4},{6,5},{7,6},{8,11},{9,8},{10,9... | collective-permute-start | bytes 786440 | tf_op jit(solution)/shard_map/ppermute | solution.py:30
  22.7 89.8 %reduce-scatter.2.cloned.1.call-start = ((), (), s32[]{:S(2)}) async-start(), calls=%async_computation.2 | async-start | bytes 2621440 | tf_op jit(solution)/shard_map/reduce_scatter | solution.py:48
  36.8 6.6 %slice-start = ((s8[7340032]{0:T(1024)(128)(4,1)}), s8[4194304]{0:T(1024)(128)(4,1)S(1)}, s32[]{:S(2)}) async-start(s8[7340032]{0:T(1024)(128)(4,1)} %bitcast.11), calls=%async_computation.3 | async-start | bytes 8388608
  36.8 6.6 %slice-start.1 = ((s8[7340032]{0:T(1024)(128)(4,1)}), s8[3145728]{0:T(1024)(128)(4,1)S(1)}, s32[]{:S(2)}) async-start(s8[7340032]{0:T(1024)(128)(4,1)} %bitcast.11), calls=%async_computation.4 | async-start | bytes 6291456
  56.5 5.9 %copy-start.3 = (bf16[256,1792]{1,0:T(8,128)(2,1)}, bf16[256,1792]{1,0:T(8,128)(2,1)S(1)}, u32[]{:S(2)}) copy-start(bf16[256,1792]{1,0:T(8,128)(2,1)S(1)} %get-tuple-element.5) | copy-start | bytes 2752516
  56.5 5.9 %copy-start.2 = (bf16[256,1792]{1,0:T(8,128)(2,1)}, bf16[256,1792]{1,0:T(8,128)(2,1)S(1)}, u32[]{:S(2)}) copy-start(bf16[256,1792]{1,0:T(8,128)(2,1)S(1)} %get-tuple-element.4) | copy-start | bytes 2752516
  68.9 6.5 %copy-start.4 = (bf16[256,1792]{1,0:T(8,128)(2,1)S(1)}, bf16[256,1792]{1,0:T(8,128)(2,1)}, u32[]{:S(2)}) copy-start(bf16[256,1792]{1,0:T(8,128)(2,1)} %copy-done.3) | copy-start | bytes 2752516
  75.4 5.4 %copy-start.1 = (bf16[256,2048]{1,0:T(8,128)(2,1)S(1)}, bf16[256,2048]{1,0:T(8,128)(2,1)}, u32[]{:S(2)}) copy-start(bf16[256,2048]{1,0:T(8,128)(2,1)} %all-gather.2.cloned.1.call-done) | copy-start | bytes 3145732
  75.4 5.4 %copy-start.5 = (f32[256,1792]{1,0:T(8,128)S(1)}, f32[256,1792]{1,0:T(8,128)}, u32[]{:S(2)}) copy-start(f32[256,1792]{1,0:T(8,128)} %convolution_multiply_fusion) | copy-start | bytes 5505028
  75.4 5.4 %copy-start.6 = (f32[256,1792]{1,0:T(8,128)S(1)}, f32[256,1792]{1,0:T(8,128)}, u32[]{:S(2)}) copy-start(f32[256,1792]{1,0:T(8,128)} %convolution_multiply_fusion.1) | copy-start | bytes 5505028
Sparse Core Ops, SparseCore 0:
  22.8 26.5 all-gather.1
  69.1 43.4 reduce-scatter.1
